TPU v7x, 32 devices: a whole 2x2x4 slice. The times are simulated.
32 devices in a mesh: rep: 8 (over y, x, core), fsdp: 4 (over z).
Axes of the slice: x: 2, y: 2, z: 4, core: 2. Of those that a mesh axis runs over, the one named last changes fastest.
Arguments:
- tokens: bfloat16 [8, 2048, 1088], P('rep', 'fsdp'), may hold values from -6 to 6
- w_qkv: bfloat16 [1088, 3264], P('fsdp'), may hold values from -0.1875 to 0.1875
- qv_bias: bfloat16 [2176], P('fsdp'), may hold values from -0.29882812 to 0.29882812
- w_out: bfloat16 [1088, 1088], P('fsdp'), may hold values from -1.5 to 1.5
- out_bias: bfloat16 [1088], P('fsdp'), may hold values from -1.796875 to 1.796875
- w_up: bfloat16 [1088, 4352], P('fsdp'), may hold values from -0.1875 to 0.1875
- up_bias: bfloat16 [4352], P('fsdp'), may hold values from -3 to 3
- w_down: bfloat16 [4352, 1088], P('fsdp'), may hold values from -0.09375 to 0.09375
- down_bias: bfloat16 [1088], P('fsdp'), may hold values from -1.796875 to 1.796875
- ln1_gain: bfloat16 [1088], P('fsdp'), may hold values from 0.099609375 to 1.8984375
- ln1_bias: bfloat16 [1088], P('fsdp'), may hold values from -3 to 3
- ln2_gain: bfloat16 [1088], P('fsdp'), may hold values from 0.099609375 to 1.8984375
- ln2_bias: bfloat16 [1088], P('fsdp'), may hold values from -3 to 3
- cotangent: bfloat16 [8, 2048, 1088], P('rep', 'fsdp'), may hold values from -6 to 6
Outputs:
- layer_out: float32 [8, 2048, 1088], P('rep', 'fsdp')
- grad_tokens: float32 [8, 2048, 1088], P('rep', 'fsdp')
- grad_w_qkv: float32 [1088, 3264], P('fsdp')
- grad_qv_bias: float32 [2176], P('fsdp')
- grad_w_out: float32 [1088, 1088], P('fsdp')
- grad_out_bias: float32 [1088], P('fsdp')
- grad_w_up: float32 [1088, 4352], P('fsdp')
- grad_up_bias: float32 [4352], P('fsdp')
- grad_w_down: float32 [4352, 1088], P('fsdp')
- grad_down_bias: float32 [1088], P('fsdp')
- grad_ln1_gain: float32 [1088], P('fsdp')
- grad_ln1_bias: float32 [1088], P('fsdp')
- grad_ln2_gain: float32 [1088], P('fsdp')
- grad_ln2_bias: float32 [1088], P('fsdp')
All inputs are finite; a program needn't handle non-finite values.
Results may differ from a plain program's by a relative error of at most 0.012.
Values may be sent and summed in bfloat16 or wider, within the bound.
No kernel may reach another device: no remote copies, remote signals or barrier semaphores. Data moves between devices by JAX's collectives and lax.ppermute only.
A program may use at most 256 MiB of HBM per device.

v0:
```python
import jax
import jax.numpy as jnp
from jax import lax
from jax.sharding import PartitionSpec as P

HD = 64
EPSILON = 1e-05


def normalize(vector):
    centre = vector - jnp.mean(vector, axis=-1, keepdims=True)
    inverse = lax.rsqrt(jnp.mean(centre * centre, axis=-1, keepdims=True) + EPSILON)
    return centre * inverse


def gelu_exact(vector):
    return jax.nn.gelu(vector, approximate=False)


def local(
    tokens,
    w_qkv,
    qv_bias,
    w_out,
    out_bias,
    w_up,
    up_bias,
    w_down,
    down_bias,
    ln1_gain,
    ln1_bias,
    ln2_gain,
    ln2_bias,
    cotangent,
):
    seq_count, local_len, features = tokens.shape
    rows = w_qkv.shape[0]
    reps = lax.axis_size("rep")
    rep_at = lax.axis_index("rep")
    everyone = ("fsdp", "rep")

    def own_piece(matrix):
        part = matrix.shape[0] // reps
        return lax.dynamic_slice_in_dim(matrix, rep_at * part, part, 0)

    def to_units(matrix):
        blocks = matrix.shape[1] // features
        return matrix.reshape(rows, blocks, features).transpose(1, 0, 2)

    def gather_all(matrix):
        return lax.all_gather(own_piece(matrix), everyone, axis=0, tiled=True)

    def from_units(units):
        blocks = units.shape[1]
        return units.transpose(0, 2, 1, 3).reshape(features, blocks * features)

    pack_one = jnp.concatenate([to_units(w_qkv), to_units(w_out)], 0)
    units_one = gather_all(pack_one.reshape(-1, features)).reshape(-1, 4, rows, features)
    units_up = gather_all(to_units(w_up).reshape(-1, features)).reshape(-1, 4, rows, features)
    down_full = gather_all(w_down)
    qkv_full = from_units(units_one[:, :3])
    out_full = from_units(units_one[:, 3:])
    up_full = from_units(units_up)
    vectors = (qv_bias, out_bias, up_bias, down_bias, ln1_gain, ln1_bias, ln2_gain, ln2_bias)
    small = lax.all_gather(jnp.concatenate(vectors), "fsdp", axis=0)
    pieces = []
    start = 0
    for vector in vectors:
        pieces.append(small[:, start : start + vector.shape[0]].reshape(-1))
        start += vector.shape[0]
    qv_full, outb_full, upb_full, downb_full, gain_one, shift_one, gain_two, shift_two = pieces
    row_count = seq_count * local_len
    total_len = local_len * lax.axis_size("fsdp")
    offset = lax.axis_index("fsdp") * local_len
    head_count = features // HD
    scale = HD ** (-0.5)
    inputs = tokens.reshape(row_count, features).astype(jnp.float32)
    normal_one, pull_one = jax.vjp(normalize, inputs)
    first = (normal_one * gain_one.astype(jnp.float32) + shift_one.astype(jnp.float32)).astype(
        jnp.bfloat16
    )
    qv_wide = qv_full.astype(jnp.float32)
    zero_keys = jnp.zeros((features,), jnp.float32)
    full_bias = jnp.concatenate([qv_wide[:features], zero_keys, qv_wide[features:]])
    mixed = (jnp.dot(first, qkv_full, preferred_element_type=jnp.float32) + full_bias).astype(
        jnp.bfloat16
    )
    queries = mixed[:, :features].reshape(seq_count, local_len, features)
    keys = mixed[:, features : 2 * features].reshape(seq_count, local_len, features)
    values = mixed[:, 2 * features :].reshape(seq_count, local_len, features)
    keys_all, values_all = (
        lax.all_gather(keys, "fsdp", axis=1, tiled=True),
        lax.all_gather(values, "fsdp", axis=1, tiled=True),
    )
    query_pos = offset + jnp.arange(local_len, dtype=jnp.int32)
    key_pos = jnp.arange(total_len, dtype=jnp.int32)
    allowed = key_pos[None, :] <= query_pos[:, None]

    def head_parts(head_index, source):
        column = head_index * HD
        return lax.dynamic_slice_in_dim(source, column, HD, 2)

    def head_scores(query_part, key_part):
        scores = (
            jnp.einsum("sqd,skd->sqk", query_part, key_part, preferred_element_type=jnp.float32)
            * scale
        )
        return jnp.where(allowed[None], scores, -1e30)

    def head_forward(head_index):
        query_part = head_parts(head_index, queries)
        key_part = head_parts(head_index, keys_all)
        value_part = head_parts(head_index, values_all)
        scores = head_scores(query_part, key_part)
        row_peak = jnp.max(scores, axis=-1, keepdims=True)
        weights = jnp.exp(scores - row_peak)
        row_total = jnp.sum(weights, axis=-1, keepdims=True)
        probabilities = (weights / row_total).astype(jnp.bfloat16)
        head_out = jnp.einsum(
            "sqk,skd->sqd", probabilities, value_part, preferred_element_type=jnp.float32
        )
        return (head_out, (row_peak + jnp.log(row_total))[..., 0])

    head_indices = jnp.arange(head_count, dtype=jnp.int32)
    per_head, logsum = lax.map(head_forward, head_indices)
    attended = per_head.transpose(1, 2, 0, 3).reshape(row_count, features).astype(jnp.bfloat16)
    branch = jnp.dot(attended, out_full, preferred_element_type=jnp.float32) + outb_full.astype(
        jnp.float32
    )
    hidden = inputs + branch
    normal_two, pull_two = jax.vjp(normalize, hidden)
    second = (normal_two * gain_two.astype(jnp.float32) + shift_two.astype(jnp.float32)).astype(
        jnp.bfloat16
    )
    upward = jnp.dot(second, up_full, preferred_element_type=jnp.float32) + upb_full.astype(
        jnp.float32
    )
    activated, pull_gelu = jax.vjp(gelu_exact, upward)
    act_low = activated.astype(jnp.bfloat16)
    result = hidden + (
        jnp.dot(act_low, down_full, preferred_element_type=jnp.float32)
        + downb_full.astype(jnp.float32)
    )
    qkv_back, out_back, up_back, down_back, gain_one_back, gain_two_back = (
        qkv_full,
        out_full,
        up_full,
        down_full,
        gain_one,
        gain_two,
    )
    upstream = cotangent.reshape(row_count, features).astype(jnp.float32)
    down_grad = cotangent.reshape(row_count, features)
    grad_down_w = jnp.einsum("rf,rd->fd", act_low, down_grad, preferred_element_type=jnp.float32)
    grad_down_b = jnp.sum(upstream, axis=0)
    grad_act = jnp.einsum("rd,fd->rf", down_grad, down_back, preferred_element_type=jnp.float32)
    (grad_upward,) = pull_gelu(grad_act)
    up_low = grad_upward.astype(jnp.bfloat16)
    grad_up_w = jnp.einsum("rd,rf->df", second, up_low, preferred_element_type=jnp.float32)
    grad_up_b = jnp.sum(up_low.astype(jnp.float32), axis=0)
    grad_second = jnp.einsum("rf,df->rd", up_low, up_back, preferred_element_type=jnp.float32)
    grad_gain_two = jnp.sum(grad_second * normal_two, axis=0)
    grad_shift_two = jnp.sum(grad_second, axis=0)
    (grad_norm_two,) = pull_two(grad_second * gain_two_back.astype(jnp.float32))
    grad_hidden = upstream + grad_norm_two
    branch_grad = grad_hidden.astype(jnp.bfloat16)
    grad_out_w = jnp.einsum("rc,rd->cd", attended, branch_grad, preferred_element_type=jnp.float32)
    grad_out_b = jnp.sum(branch_grad.astype(jnp.float32), axis=0)
    grad_att = jnp.einsum("rd,cd->rc", branch_grad, out_back, preferred_element_type=jnp.float32)
    grad_att = grad_att.astype(jnp.bfloat16).reshape(seq_count, local_len, features)

    def head_backward(head_pair):
        head_index, head_logsum = head_pair
        query_part = head_parts(head_index, queries)
        key_part = head_parts(head_index, keys_all)
        value_part = head_parts(head_index, values_all)
        grad_part = head_parts(head_index, grad_att)
        scores = head_scores(query_part, key_part)
        probabilities = jnp.exp(scores - head_logsum[..., None])
        grad_probs = jnp.einsum(
            "sqd,skd->sqk", grad_part, value_part, preferred_element_type=jnp.float32
        )
        inner_sum = jnp.sum(probabilities * grad_probs, axis=-1, keepdims=True)
        grad_scores = (probabilities * (grad_probs - inner_sum)).astype(jnp.bfloat16)
        grad_query = (
            jnp.einsum("sqk,skd->sqd", grad_scores, key_part, preferred_element_type=jnp.float32)
            * scale
        )
        grad_key = (
            jnp.einsum("sqk,sqd->skd", grad_scores, query_part, preferred_element_type=jnp.float32)
            * scale
        )
        grad_value = jnp.einsum(
            "sqk,sqd->skd",
            probabilities.astype(jnp.bfloat16),
            grad_part,
            preferred_element_type=jnp.float32,
        )
        return (grad_query, grad_key, grad_value)

    query_grads, key_grads, value_grads = lax.map(head_backward, (head_indices, logsum))
    query_grads = query_grads.transpose(1, 2, 0, 3).reshape(seq_count, local_len, features)
    key_grads = key_grads.transpose(1, 2, 0, 3).reshape(seq_count, total_len, features)
    value_grads = value_grads.transpose(1, 2, 0, 3).reshape(seq_count, total_len, features)
    own_keys, own_values = (
        lax.psum_scatter(key_grads.astype(jnp.bfloat16), "fsdp", scatter_dimension=1, tiled=True),
        lax.psum_scatter(value_grads.astype(jnp.bfloat16), "fsdp", scatter_dimension=1, tiled=True),
    )
    mixed_grad = jnp.concatenate([query_grads.astype(jnp.bfloat16), own_keys, own_values], axis=-1)
    mixed_grad = mixed_grad.reshape(row_count, 3 * features)
    grad_qkv_w = jnp.einsum("rd,re->de", first, mixed_grad, preferred_element_type=jnp.float32)
    column_sums = jnp.sum(mixed_grad.astype(jnp.float32), axis=0)
    grad_qv_b = jnp.concatenate([column_sums[:features], column_sums[2 * features :]])
    grad_first = jnp.einsum("re,de->rd", mixed_grad, qkv_back, preferred_element_type=jnp.float32)
    grad_gain_one = jnp.sum(grad_first * normal_one, axis=0)
    grad_shift_one = jnp.sum(grad_first, axis=0)
    (grad_norm_one,) = pull_one(grad_first * gain_one_back.astype(jnp.float32))
    grad_inputs = grad_hidden + grad_norm_one
    fsdp = lax.axis_size("fsdp")

    def grad_units(matrix):
        blocks = matrix.shape[1] // features
        return (
            matrix.astype(jnp.bfloat16).reshape(fsdp, rows, blocks, features).transpose(0, 2, 1, 3)
        )

    def reduce_all(matrix):
        part = lax.psum_scatter(matrix, everyone, scatter_dimension=0, tiled=True)
        return lax.all_gather(part, "rep", axis=0, tiled=True)

    def own_matrix(units):
        blocks = units.shape[0] // rows
        wide = units.reshape(blocks, rows, features).transpose(1, 0, 2)
        return wide.reshape(rows, blocks * features).astype(jnp.float32)

    down_own = reduce_all(grad_down_w.astype(jnp.bfloat16)).astype(jnp.float32)
    up_own = own_matrix(reduce_all(grad_units(grad_up_w).reshape(-1, features)))
    packed = jnp.concatenate([grad_units(grad_qkv_w), grad_units(grad_out_w)], 1)
    one_own = reduce_all(packed.reshape(-1, features))
    qkv_own = own_matrix(one_own[: 3 * rows])
    out_own = own_matrix(one_own[3 * rows :])
    small_grads = (
        grad_qv_b,
        grad_out_b,
        grad_up_b,
        grad_down_b,
        grad_gain_one,
        grad_shift_one,
        grad_gain_two,
        grad_shift_two,
    )
    stacked = jnp.concatenate([g.reshape(fsdp, -1) for g in small_grads], 1)
    stacked = lax.psum(stacked, ("rep", "fsdp"))
    mine = lax.dynamic_index_in_dim(stacked, lax.axis_index("fsdp"), 0, keepdims=False)
    small_own = []
    start = 0
    for g in small_grads:
        width = g.shape[0] // fsdp
        small_own.append(mine[start : start + width])
        start += width
    return (
        result.reshape(seq_count, local_len, features),
        grad_inputs.reshape(seq_count, local_len, features),
        qkv_own,
        small_own[0],
        out_own,
        small_own[1],
        up_own,
        small_own[2],
        down_own,
        small_own[3],
        small_own[4],
        small_own[5],
        small_own[6],
        small_own[7],
    )


def solution(mesh):
    return jax.shard_map(
        local,
        mesh=mesh,
        in_specs=(
            P("rep", "fsdp", None),
            P("fsdp", None),
            P("fsdp"),
            P("fsdp", None),
            P("fsdp"),
            P("fsdp", None),
            P("fsdp"),
            P("fsdp", None),
            P("fsdp"),
            P("fsdp"),
            P("fsdp"),
            P("fsdp"),
            P("fsdp"),
            P("rep", "fsdp", None),
        ),
        out_specs=(
            P("rep", "fsdp", None),
            P("rep", "fsdp", None),
            P("fsdp", None),
            P("fsdp"),
            P("fsdp", None),
            P("fsdp"),
            P("fsdp", None),
            P("fsdp"),
            P("fsdp", None),
            P("fsdp"),
            P("fsdp"),
            P("fsdp"),
            P("fsdp"),
            P("fsdp"),
        ),
        check_vma=False,
    )
```

profile of v0, /device:TPU:0, one launch (start us, length us, event | category | flops | bytes accessed | tf_op | source)
XLA Modules:
  0.0 1485.0 jit_solution(5618912969653301980)
XLA Ops:
  7.3 5.9 reshape.469
  14.2 4.4 pad_maximum_fusion.1
  22.1 6.3 reshape.476
  33.1 21.1 %all-reduce = bf16[13056]{0:T(1024)(128)(2,1)S(1)} all-reduce(bf16[13056]{0:T(1024)(128)(2,1)S(1)} %dynamic-update-slice), channel_id=2, replica_groups=mesh['rep'=8,'fsdp'=4] {'fsdp'}, use_global_device_ids=true, to_apply=%add | all-reduce | flops 13056 | bytes 52224
  58.5 50.7 %all-gather.12.cloned.1.call-done = bf16[4352,1088]{1,0:T(8,128)(2,1)} async-done(((bf16[136,1088]{1,0:T(8,128)(2,1)}), bf16[4352,1088]{1,0:T(8,128)(2,1)}) %all-gather.12.cloned.1.call-update) | async-done | bytes 9469968 | tf_op jit(solution)/shard_map/all_gather | solution.py:51
  109.2 3.7 slice.164
  112.9 10.9 copy.91
  123.8 19.2 %reshape.472 = bf16[1088,3264]{1,0:T(8,128)(2,1)} reshape(bf16[4,272,3,1088]{3,2,1,0:T(4,128)(2,1)} %bitcast.241) | data formatting | bytes 14204928 | tf_op jit(solution)/shard_map/reshape | solution.py:55
  143.0 8.3 add_convert_fusion
  155.3 3.4 slice.171
  159.4 35.9 %all-gather.14.cloned.1.call-done = bf16[4352,1088]{1,0:T(8,128)(2,1)} async-done(((bf16[136,1088]{1,0:T(8,128)(2,1)}), bf16[4352,1088]{1,0:T(8,128)(2,1)}) %all-gather.14.cloned.1.call-update) | async-done | bytes 9469968 | tf_op jit(solution)/shard_map/all_gather | solution.py:51
  195.3 9.7 copy.92
  205.0 16.7 %reshape.479 = bf16[1088,4352]{1,0:T(8,128)(2,1)} reshape(bf16[4,272,4,1088]{3,2,1,0:T(4,128)(2,1)} %bitcast.240) | data formatting | bytes 18939904 | tf_op jit(solution)/shard_map/reshape | solution.py:55
  221.6 59.5 %all-gather.24.cloned.1.call-done = bf16[2048,1088]{0,1:T(8,128)(2,1)} async-done(((bf16[512,1088]{0,1:T(8,128)(2,1)}), bf16[2048,1088]{0,1:T(8,128)(2,1)}) %all-gather.24.cloned.1.call-update) | async-done | bytes 4456464 | tf_op jit(solution)/shard_map/all_gather | solution.py:92
  281.1 6.4 copy.73
  287.5 79.1 %all-gather.26.cloned.1.call-done = bf16[2048,1088]{0,1:T(8,128)(2,1)} async-done(((bf16[512,1088]{0,1:T(8,128)(2,1)}), bf16[2048,1088]{0,1:T(8,128)(2,1)}) %all-gather.26.cloned.1.call-update) | async-done | bytes 4456464 | tf_op jit(solution)/shard_map/all_gather | solution.py:93
  366.6 6.4 copy.74
  374.2 118.2 %while.28 = (s32[]{:T(128)}, bf16[17,1,512,64]{2,3,1,0:T(8,128)(2,1)}, f32[17,1,512]{2,1,0:T(1,128)S(1)}, s32[17]{0:T(128)S(1)}, bf16[1,512,1088]{2,1,0:T(8,128)...) while((s32[]{:T(128)}, ...), condition=%wide.region_5.6_spmd.clone, body=%wide.region_2.5_spmd.clone.sunk | while | flops 277872128 | bytes 13917879 | solution.py:125
  447.8 3.0 fusion.129
  492.4 4.2 fusion.91
  497.9 32.5 %multiply_convert_fusion.1 = (bf16[512,4352]{1,0:T(8,128)(2,1)}, f32[512,4352]{1,0:T(8,128)}, f32[512,4352]{1,0:T(8,128)}) fusion(f32[4352]{0:T(1024)S(1)} %reshape.501, bf16[1088,4352]{1,0:T(8,128)(2,1)} %reshape.479, f32[512,1088]{0,1:T(8,128)S(1)} %get-tuple-element.318, f32[1088]{0:T(1024)S(1)} %reshape.500, f32[1088]{0:T(1024)S(1)} %reshape.499, ...), kind=kOutput, calls=%fused_computation.72 | convolution fusion | flops 4998463488 | bytes 34010624 | tf_op jit(solution)/shard_map/dot_general | solution.py:135
  530.5 18.5 %convert_reduce_fusion = (f32[4352]{0:T(1024)}, bf16[512,4352]{1,0:T(8,128)(2,1)}) fusion(f32[512,4352]{1,0:T(8,128)} %get-tuple-element.297, bf16[4352,1088]{1,0:T(8,128)(2,1)} %all-gather.16.cloned.1.call-done, bf16[1,512,1088]{1,2,0:T(8,128)(2,1)S(1)} %copy-done.12, f32[512,4352]{1,0:T(8,128)} %get-tuple-element.319, f32[4352]{0:T(1024)S(1)} %reshape.501), kind=kOutput, calls=%fused_computation.71 | convolution fusion | flops 4886491136 | bytes 32901120 | tf_op jit(solution)/shard_map/rd,fd->rf/dot_general | solution.py:156
  549.0 10.0 multiply_reduce_fusion.1
  566.4 225.5 %while.29 = (s32[]{:T(128)}, bf16[17,1,512,64]{2,3,1,0:T(8,128)(2,1)}, bf16[17,1,2048,64]{2,3,1,0:T(8,128)(2,1)}, bf16[17,1,2048,64]{2,3,1,0:T(8,128)(2,1)}, s32...) while((s32[]{:T(128)}, ...), condition=%wide.region_12.13_spmd.clone, body=%wide.region_10.12_spmd.clone.sunk | while | flops 681737728 | bytes 34619096 | solution.py:201
  793.6 10.0 convolution_convert_fusion.1
  803.6 18.7 %reshape.494 = bf16[4,272,4,1088]{3,2,1,0:T(4,128)(2,1)} reshape(bf16[1088,4352]{1,0:T(8,128)(2,1)} %convolution_convert_fusion.1) | data formatting | bytes 18939904 | tf_op jit(solution)/shard_map/reshape | solution.py:224
  822.3 8.9 copy.84
  832.4 11.8 convolution_convert_fusion
  845.5 4.4 convolution_convert_fusion.3
  849.8 7.9 copy.81
  857.8 13.8 reduce-scatter.12.cloned.1.call-done
  871.6 83.9 %reduce-scatter.14.cloned.1.call-done = bf16[1,512,1088]{1,2,0:T(8,128)(2,1)} async-done(((bf16[1,2048,1088]{1,2,0:T(8,128)(2,1)}), bf16[1,512,1088]{1,2,0:T(8,128)(2,1)}) %reduce-scatter.14.cloned.1.call-update) | async-done | bytes 1114128 | tf_op jit(solution)/shard_map/reduce_scatter | solution.py:207
  955.5 8.3 convolution_convert_fusion.2
  963.8 19.8 %reshape.485 = bf16[4,272,3,1088]{3,2,1,0:T(4,128)(2,1)} reshape(bf16[1088,3264]{1,0:T(8,128)(2,1)} %convolution_convert_fusion.2) | data formatting | bytes 14204928 | tf_op jit(solution)/shard_map/reshape | solution.py:224
  983.5 13.9 pad_maximum_fusion
  997.4 9.0 copy.82
  1006.5 88.7 %reduce-scatter.18.cloned.1.call-done = bf16[136,1088]{1,0:T(8,128)(2,1)} async-done(((bf16[4352,1088]{1,0:T(8,128)(2,1)}), bf16[136,1088]{1,0:T(8,128)(2,1)}) %reduce-scatter.18.cloned.1.call-update) | async-done | bytes 295952
  1095.3 138.1 %reduce-scatter.20.cloned.1.call-done = bf16[136,1088]{1,0:T(8,128)(2,1)} async-done(((bf16[4352,1088]{1,0:T(8,128)(2,1)}), bf16[136,1088]{1,0:T(8,128)(2,1)}) %reduce-scatter.20.cloned.1.call-update) | async-done | bytes 295952
  1233.7 137.7 %reduce-scatter.16.cloned.1.call-done = bf16[136,1088]{1,0:T(8,128)(2,1)} async-done(((bf16[4352,1088]{1,0:T(8,128)(2,1)}), bf16[136,1088]{1,0:T(8,128)(2,1)}) %reduce-scatter.16.cloned.1.call-update) | async-done | bytes 295952
  1371.4 13.9 fusion.57
  1388.1 8.2 fusion.83
  1401.1 40.4 %psum.7 = f32[4,3264]{1,0:T(4,128)S(1)} all-reduce(f32[4,3264]{1,0:T(4,128)S(1)} %concatenate.34), channel_id=1, replica_groups=mesh['rep'=8,'fsdp'=4] {'rep','fsdp'}, use_global_device_ids=true, to_apply=%region_26.27 | all-reduce | flops 13056 | bytes 104448 | tf_op jit(solution)/shard_map/psum | solution.py:253
  1445.5 4.2 copy.85
  1449.7 6.5 reshape.504
  1456.3 4.3 convert_element_type.291
  1460.6 4.0 all-gather.18.cloned.1.call-done
  1466.1 3.2 copy.93
  1469.3 6.7 reshape.503
  (426 shorter events, 364.6 us)
Async XLA Ops:
  7.2 146.7 %copy-start = (bf16[1088,1088]{1,0:T(8,128)(2,1)S(1)}, bf16[1088,1088]{1,0:T(8,128)(2,1)}, u32[]{:S(2)}) copy-start(bf16[1088,1088]{1,0:T(8,128)(2,1)} %param.25) | copy-start | bytes 7102468
  7.2 6.0 copy-start.20
  7.2 102.0 %all-gather.12.cloned.1.call-start = ((), (), s32[]{:S(2)}) async-start(), calls=%async_computation.5 | async-start | bytes 10340352 | tf_op jit(solution)/shard_map/all_gather | solution.py:51
  22.0 173.3 %all-gather.14.cloned.1.call-start = ((), (), s32[]{:S(2)}) async-start(), calls=%async_computation.6 | async-start | bytes 10340352 | tf_op jit(solution)/shard_map/all_gather | solution.py:51
  28.4 4.2 copy-start.35
  28.4 4.2 copy-start.36
  28.4 4.2 copy-start.37
  28.4 4.3 copy-start.38
  28.4 4.2 copy-start.39
  28.4 4.2 copy-start.40
  28.4 4.2 copy-start.41
  28.4 4.2 copy-start.42
  31.3 249.8 %all-gather.24.cloned.1.call-start = ((), (), s32[]{:S(2)}) async-start(), calls=%async_computation.13 | async-start | bytes 5570560 | tf_op jit(solution)/shard_map/all_gather | solution.py:92
  55.0 88.0 %copy-start.21 = (f32[1088]{0:T(1024)}, f32[1088]{0:T(1024)S(1)}, u32[]{:S(2)}) copy-start(f32[1088]{0:T(1024)S(1)} %reshape.496) | copy-start | bytes 13060
  55.3 87.7 %copy-start.33 = (f32[1088]{0:T(1024)}, f32[1088]{0:T(1024)S(1)}, u32[]{:S(2)}) copy-start(f32[1088]{0:T(1024)S(1)} %reshape.497) | copy-start | bytes 13060
  56.9 86.2 %copy-start.23 = (f32[512]{0:T(512)}, f32[512]{0:T(512)S(1)}, u32[]{:S(2)}) copy-start(f32[512]{0:T(512)S(1)} %broadcast_multiply_fusion.1) | copy-start | bytes 6148
  58.5 54.4 %copy-start.27 = (f32[512]{0:T(512)}, f32[512]{0:T(512)S(1)}, u32[]{:S(2)}) copy-start(f32[512]{0:T(512)S(1)} %fusion.64) | copy-start | bytes 6148
  58.5 84.5 %copy-start.29 = (f32[512]{0:T(512)}, f32[512]{0:T(512)S(1)}, u32[]{:S(2)}) copy-start(f32[512]{0:T(512)S(1)} %fusion.77) | copy-start | bytes 6148
  153.2 213.4 %all-gather.26.cloned.1.call-start = ((), (), s32[]{:S(2)}) async-start(), calls=%async_computation.14 | async-start | bytes 5570560 | tf_op jit(solution)/shard_map/all_gather | solution.py:93
  153.8 376.6 %all-gather.16.cloned.1.call-start = ((), (), s32[]{:S(2)}) async-start(), calls=%async_computation.7 | async-start | bytes 10340352 | tf_op jit(solution)/shard_map/all_gather | solution.py:51
  154.6 4.1 copy-start.11
  154.6 717.0 %reduce-scatter.12.cloned.1.call-start = ((), (), s32[]{:S(2)}) async-start(), calls=%async_computation.8 | async-start | bytes 5570560 | tf_op jit(solution)/shard_map/reduce_scatter | solution.py:206
  374.2 118.2 %copy-start.4 = (bf16[1,512,1088]{1,2,0:T(8,128)(2,1)S(1)}, bf16[1,512,1088]{1,2,0:T(8,128)(2,1)}, u32[]{:S(2)}) copy-start(bf16[1,512,1088]{1,2,0:T(8,128)(2,1)} %param.18) | copy-start | bytes 3342340
  492.4 4.2 copy-start.10
  497.9 32.5 %copy-start.12 = (bf16[1,512,1088]{1,2,0:T(8,128)(2,1)S(1)}, bf16[1,512,1088]{1,2,0:T(8,128)(2,1)}, u32[]{:S(2)}) copy-start(bf16[1,512,1088]{1,2,0:T(8,128)(2,1)} %param.31) | copy-start | bytes 3342340
  530.4 18.5 %copy-start.8 = (f32[512,1088]{0,1:T(8,128)S(1)}, f32[512,1088]{0,1:T(8,128)}, u32[]{:S(2)}) copy-start(f32[512,1088]{0,1:T(8,128)} %copy-done.7) | copy-start | bytes 6684676
  559.7 5.6 copy-start.2
  559.7 3.0 copy-start.16
  559.7 5.6 copy-start.31
  560.7 4.6 copy-start.18
  792.0 163.5 %reduce-scatter.14.cloned.1.call-start = ((), (), s32[]{:S(2)}) async-start(), calls=%async_computation.9 | async-start | bytes 5570560 | tf_op jit(solution)/shard_map/reduce_scatter | solution.py:207
  792.7 302.5 %reduce-scatter.18.cloned.1.call-start = ((), (), s32[]{:S(2)}) async-start(), calls=%async_computation.16 | async-start | bytes 10340352
  831.2 402.2 %reduce-scatter.20.cloned.1.call-start = ((), (), s32[]{:S(2)}) async-start(), calls=%async_computation.17 | async-start | bytes 10340352
  844.2 527.1 %reduce-scatter.16.cloned.1.call-start = ((), (), s32[]{:S(2)}) async-start(), calls=%async_computation.15 | async-start | bytes 10340352
  849.8 105.6 %copy-start.5 = (bf16[1,512,1088]{1,2,0:T(8,128)(2,1)S(1)}, bf16[1,512,1088]{1,2,0:T(8,128)(2,1)}, u32[]{:S(2)}) copy-start(bf16[1,512,1088]{1,2,0:T(8,128)(2,1)} %param.18) | copy-start | bytes 3342340
  849.8 105.6 %copy-start.22 = (f32[1088]{0:T(1024)S(1)}, f32[1088]{0:T(1024)}, u32[]{:S(2)}) copy-start(f32[1088]{0:T(1024)} %copy-done.21) | copy-start | bytes 13060
  849.8 105.6 %copy-start.24 = (f32[512]{0:T(512)S(1)}, f32[512]{0:T(512)}, u32[]{:S(2)}) copy-start(f32[512]{0:T(512)} %copy-done.23) | copy-start | bytes 6148
  849.8 105.6 %copy-start.30 = (f32[512]{0:T(512)S(1)}, f32[512]{0:T(512)}, u32[]{:S(2)}) copy-start(f32[512]{0:T(512)} %copy-done.29) | copy-start | bytes 6148
  849.8 105.6 %copy-start.34 = (f32[1088]{0:T(1024)S(1)}, f32[1088]{0:T(1024)}, u32[]{:S(2)}) copy-start(f32[1088]{0:T(1024)} %copy-done.33) | copy-start | bytes 13060
  1006.4 227.2 %copy-start.25 = (f32[4,272]{1,0:T(4,128)S(1)}, f32[4,272]{1,0:T(4,128)}, u32[]{:S(2)}) copy-start(f32[4,272]{1,0:T(4,128)} %get-tuple-element.307) | copy-start | bytes 13060
  1006.5 437.0 %all-gather.20.cloned.1.call-start = ((), (), s32[]{:S(2)}) async-start(), calls=%async_computation.11 | async-start | bytes 2820096 | tf_op jit(solution)/shard_map/all_gather | solution.py:229
  1095.2 361.0 %all-gather.22.cloned.1.call-start = ((), (), s32[]{:S(2)}) async-start(), calls=%async_computation.12 | async-start | bytes 2820096 | tf_op jit(solution)/shard_map/all_gather | solution.py:229
  1233.4 231.2 %all-gather.18.cloned.1.call-start = ((), (), s32[]{:S(2)}) async-start(), calls=%async_computation.10 | async-start | bytes 2820096 | tf_op jit(solution)/shard_map/all_gather | solution.py:229
  1371.4 14.1 copy-start.26
  1371.4 14.2 copy-start.17
  1388.1 8.3 copy-start.28
  1388.1 8.3 copy-start.6
  1469.3 8.9 copy-start.1
  (10 other events, 16.7 us)
Sparse Core Ops, SparseCore 0:
  22.1 87.0 all-gather.11
  112.7 82.5 all-gather.13
  197.5 83.5 all-gather.23
  283.1 83.4 all-gather.25
  369.4 82.4 all-gather.15
  792.1 79.4 reduce-scatter.11
  873.9 81.5 reduce-scatter.13
  961.6 133.5 reduce-scatter.17
  1101.3 132.0 reduce-scatter.19
  1239.3 131.9 reduce-scatter.15
  1373.3 28.4 all-gather.19
  1403.5 29.6 all-gather.21
  1435.1 29.4 all-gather.17
where the time goes:
time: 1500 us; the launch traced here: 1480 us
  waiting for transfers between devices  693 us (46%)
  matrix products  414 us (28%)
  local copies, waits for them, and re-layouts  220 us (15%)
  blocking collectives  61.5 us (4%)
  other arithmetic  57.4 us (4%)
  loops' own time  23 us (2%)
  between operations  15.4 us (1%)
    unnamed x16, waiting for transfers between devices  366 us
    all_gather x3, waiting for transfers between devices, gather_all(): return lax.all_gather(own_piece(matrix), everyone, axis=0, tiled=True)  86.7 us
    reduce_scatter x1, waiting for transfers between devices, local(): lax.psum_scatter(value_grads.astype(jnp.bfloat16), 'fsdp', scatter_dimens...  83.9 us
    dot_general x34, matrix products, head_scores(): jnp.einsum('sqd,skd->sqk', query_part, key_part, preferred_element_type=j...  83.4 us
    all_gather x1, waiting for transfers between devices, local(): lax.all_gather(values, 'fsdp', axis=1, tiled=True)  79.1 us
    all_gather x1, waiting for transfers between devices, local(): lax.all_gather(keys, 'fsdp', axis=1, tiled=True)  59.5 us
    dot_general x17, matrix products, head_forward(): jnp.einsum('sqk,skd->sqd', probabilities, value_part, preferred_element_t...  48.9 us
    reshape x3, local copies, waits for them, and re-layouts, grad_units(): matrix.astype(jnp.bfloat16).reshape(fsdp, rows, blocks, features)  47.3 us
  transfers between devices with their start and end apart: 13, of which 10 were waited for; matrix products, arithmetic and copies ran while one was open for 27% of the time, Pallas kernels for 0%

commit v1 on v0

--- a/solution.py
+++ b/solution.py
@@ -250,7 +250,7 @@
         grad_shift_two,
     )
     stacked = jnp.concatenate([g.reshape(fsdp, -1) for g in small_grads], 1)
-    stacked = lax.psum(stacked, ("rep", "fsdp"))
+    stacked = jnp.sum(lax.all_gather(stacked, ("rep", "fsdp")), axis=0)
     mine = lax.dynamic_index_in_dim(stacked, lax.axis_index("fsdp"), 0, keepdims=False)
     small_own = []
     start = 0

time: 1500 us -> 1550 us (1.033)
  waiting for transfers between devices: 693 us -> 787 us
  blocking collectives: 61.5 us -> 21.1 us
    all_gather x3, waiting for transfers between devices: 4.04 us -> 72 us  [reduce_all(): return lax.all_gather(part, 'rep', axis=0, tiled=True)]
    all_gather x0 -> x1, waiting for transfers between devices: none -> 43.7 us  [local(): stacked = jnp.sum(lax.all_gather(stacked, ('rep', 'fsdp')), axis=0)]
    psum x1 -> x0, blocking collectives: 40.4 us -> none  [local(): stacked = lax.psum(stacked, ('rep', 'fsdp'))]
    unnamed x16 -> x17, waiting for transfers between devices: 366 us -> 349 us
    unnamed x95 -> x89, local copies, waits for them, and re-layouts: 32.7 us -> 33.3 us
  transfers between devices with their start and end apart: 13 -> 14, of which waited for: 10 -> 13; matrix products, arithmetic and copies ran while one was open for 27% -> 27% of each run, Pallas kernels for 0% -> 0%
where the time goes in v1:
time: 1550 us; the launch traced here: 1540 us
  waiting for transfers between devices  787 us (51%)
  matrix products  412 us (27%)
  local copies, waits for them, and re-layouts  221 us (14%)
  other arithmetic  59.4 us (4%)
  loops' own time  23 us (1%)
  blocking collectives  21.1 us (1%)
    unnamed x17, waiting for transfers between devices  349 us
    all_gather x3, waiting for transfers between devices, gather_all(): return lax.all_gather(own_piece(matrix), everyone, axis=0, tiled=True)  86.6 us
    reduce_scatter x1, waiting for transfers between devices, local(): lax.psum_scatter(value_grads.astype(jnp.bfloat16), 'fsdp', scatter_dimens...  83.9 us
    dot_general x34, matrix products, head_scores(): jnp.einsum('sqd,skd->sqk', query_part, key_part, preferred_element_type=j...  83.4 us
    all_gather x1, waiting for transfers between devices, local(): lax.all_gather(values, 'fsdp', axis=1, tiled=True)  79.1 us
    all_gather x3, waiting for transfers between devices, reduce_all(): return lax.all_gather(part, 'rep', axis=0, tiled=True)  72 us
    all_gather x1, waiting for transfers between devices, local(): lax.all_gather(keys, 'fsdp', axis=1, tiled=True)  59.5 us
    dot_general x17, matrix products, head_forward(): jnp.einsum('sqk,skd->sqd', probabilities, value_part, preferred_element_t...  48.7 us
  transfers between devices with their start and end apart: 14, of which 13 were waited for; matrix products, arithmetic and copies ran while one was open for 27% of the time, Pallas kernels for 0%

profile of v1, /device:TPU:0, one launch (start us, length us, event | category | flops | bytes accessed | tf_op | source)
XLA Modules:
  0.0 1541.3 jit_solution(3148637956026607438)
XLA Ops:
  7.3 5.9 reshape.469
  14.2 4.4 pad_maximum_fusion.1
  22.1 6.3 reshape.476
  33.1 21.1 %all-reduce = bf16[13056]{0:T(1024)(128)(2,1)S(1)} all-reduce(bf16[13056]{0:T(1024)(128)(2,1)S(1)} %dynamic-update-slice), channel_id=2, replica_groups=mesh['rep'=8,'fsdp'=4] {'fsdp'}, use_global_device_ids=true, to_apply=%add | all-reduce | flops 13056 | bytes 52224
  58.5 50.7 %all-gather.15.cloned.1.call-done = bf16[4352,1088]{1,0:T(8,128)(2,1)} async-done(((bf16[136,1088]{1,0:T(8,128)(2,1)}), bf16[4352,1088]{1,0:T(8,128)(2,1)}) %all-gather.15.cloned.1.call-update) | async-done | bytes 9469968 | tf_op jit(solution)/shard_map/all_gather | solution.py:51
  109.2 3.7 slice.164
  112.9 10.9 copy.91
  123.8 19.2 %reshape.472 = bf16[1088,3264]{1,0:T(8,128)(2,1)} reshape(bf16[4,272,3,1088]{3,2,1,0:T(4,128)(2,1)} %bitcast.242) | data formatting | bytes 14204928 | tf_op jit(solution)/shard_map/reshape | solution.py:55
  143.0 8.3 add_convert_fusion
  155.3 3.4 slice.171
  159.4 35.9 %all-gather.17.cloned.1.call-done = bf16[4352,1088]{1,0:T(8,128)(2,1)} async-done(((bf16[136,1088]{1,0:T(8,128)(2,1)}), bf16[4352,1088]{1,0:T(8,128)(2,1)}) %all-gather.17.cloned.1.call-update) | async-done | bytes 9469968 | tf_op jit(solution)/shard_map/all_gather | solution.py:51
  195.3 9.7 copy.92
  205.0 16.7 %reshape.479 = bf16[1088,4352]{1,0:T(8,128)(2,1)} reshape(bf16[4,272,4,1088]{3,2,1,0:T(4,128)(2,1)} %bitcast.241) | data formatting | bytes 18939904 | tf_op jit(solution)/shard_map/reshape | solution.py:55
  221.6 59.5 %all-gather.27.cloned.1.call-done = bf16[2048,1088]{0,1:T(8,128)(2,1)} async-done(((bf16[512,1088]{0,1:T(8,128)(2,1)}), bf16[2048,1088]{0,1:T(8,128)(2,1)}) %all-gather.27.cloned.1.call-update) | async-done | bytes 4456464 | tf_op jit(solution)/shard_map/all_gather | solution.py:92
  281.1 6.4 copy.73
  287.5 79.1 %all-gather.29.cloned.1.call-done = bf16[2048,1088]{0,1:T(8,128)(2,1)} async-done(((bf16[512,1088]{0,1:T(8,128)(2,1)}), bf16[2048,1088]{0,1:T(8,128)(2,1)}) %all-gather.29.cloned.1.call-update) | async-done | bytes 4456464 | tf_op jit(solution)/shard_map/all_gather | solution.py:93
  366.6 6.4 copy.74
  374.2 118.0 %while.28 = (s32[]{:T(128)}, bf16[17,1,512,64]{2,3,1,0:T(8,128)(2,1)}, f32[17,1,512]{2,1,0:T(1,128)S(1)}, s32[17]{0:T(128)S(1)}, bf16[1,512,1088]{2,1,0:T(8,128)...) while((s32[]{:T(128)}, ...), condition=%wide.region_5.6_spmd.clone, body=%wide.region_2.5_spmd.clone.sunk | while | flops 277872128 | bytes 13917879 | solution.py:125
  492.2 4.2 fusion.91
  497.8 32.4 %multiply_convert_fusion.1 = (bf16[512,4352]{1,0:T(8,128)(2,1)}, f32[512,4352]{1,0:T(8,128)}, f32[512,4352]{1,0:T(8,128)}) fusion(f32[4352]{0:T(1024)S(1)} %reshape.501, bf16[1088,4352]{1,0:T(8,128)(2,1)} %reshape.479, f32[512,1088]{0,1:T(8,128)S(1)} %get-tuple-element.318, f32[1088]{0:T(1024)S(1)} %reshape.500, f32[1088]{0:T(1024)S(1)} %reshape.499, ...), kind=kOutput, calls=%fused_computation.72 | convolution fusion | flops 4998463488 | bytes 34010624 | tf_op jit(solution)/shard_map/dot_general | solution.py:135
  530.3 18.0 %convert_reduce_fusion = (f32[4352]{0:T(1024)S(1)}, bf16[512,4352]{1,0:T(8,128)(2,1)}) fusion(f32[512,4352]{1,0:T(8,128)} %get-tuple-element.297, bf16[4352,1088]{1,0:T(8,128)(2,1)} %all-gather.19.cloned.1.call-done, bf16[1,512,1088]{1,2,0:T(8,128)(2,1)S(1)} %copy-done.12, f32[512,4352]{1,0:T(8,128)} %get-tuple-element.319, f32[4352]{0:T(1024)S(1)} %reshape.501), kind=kOutput, calls=%fused_computation.71 | convolution fusion | flops 4886491136 | bytes 32901120 | tf_op jit(solution)/shard_map/rd,fd->rf/dot_general | solution.py:156
  548.2 10.0 multiply_reduce_fusion.1
  565.7 225.4 %while.29 = (s32[]{:T(128)}, bf16[17,1,512,64]{2,3,1,0:T(8,128)(2,1)}, bf16[17,1,2048,64]{2,3,1,0:T(8,128)(2,1)}, bf16[17,1,2048,64]{2,3,1,0:T(8,128)(2,1)}, s32...) while((s32[]{:T(128)}, ...), condition=%wide.region_12.13_spmd.clone, body=%wide.region_10.12_spmd.clone.sunk | while | flops 681737728 | bytes 34619096 | solution.py:201
  792.8 10.0 convolution_convert_fusion.1
  802.8 18.7 %reshape.494 = bf16[4,272,4,1088]{3,2,1,0:T(4,128)(2,1)} reshape(bf16[1088,4352]{1,0:T(8,128)(2,1)} %convolution_convert_fusion.1) | data formatting | bytes 18939904 | tf_op jit(solution)/shard_map/reshape | solution.py:224
  821.5 8.9 copy.84
  831.6 11.8 convolution_convert_fusion
  844.6 4.4 convolution_convert_fusion.3
  849.0 7.9 copy.81
  857.0 13.8 reduce-scatter.12.cloned.1.call-done
  870.8 83.9 %reduce-scatter.14.cloned.1.call-done = bf16[1,512,1088]{1,2,0:T(8,128)(2,1)} async-done(((bf16[1,2048,1088]{1,2,0:T(8,128)(2,1)}), bf16[1,512,1088]{1,2,0:T(8,128)(2,1)}) %reduce-scatter.14.cloned.1.call-update) | async-done | bytes 1114128 | tf_op jit(solution)/shard_map/reduce_scatter | solution.py:207
  954.7 8.3 convolution_convert_fusion.2
  963.0 19.8 %reshape.485 = bf16[4,272,3,1088]{3,2,1,0:T(4,128)(2,1)} reshape(bf16[1088,3264]{1,0:T(8,128)(2,1)} %convolution_convert_fusion.2) | data formatting | bytes 14204928 | tf_op jit(solution)/shard_map/reshape | solution.py:224
  982.8 13.9 pad_maximum_fusion
  996.7 9.0 copy.82
  1009.7 8.0 fusion.83
  1023.1 71.4 %reduce-scatter.18.cloned.1.call-done = bf16[136,1088]{1,0:T(8,128)(2,1)} async-done(((bf16[4352,1088]{1,0:T(8,128)(2,1)}), bf16[136,1088]{1,0:T(8,128)(2,1)}) %reduce-scatter.18.cloned.1.call-update) | async-done | bytes 295952
  1094.6 138.1 %reduce-scatter.20.cloned.1.call-done = bf16[136,1088]{1,0:T(8,128)(2,1)} async-done(((bf16[4352,1088]{1,0:T(8,128)(2,1)}), bf16[136,1088]{1,0:T(8,128)(2,1)}) %reduce-scatter.20.cloned.1.call-update) | async-done | bytes 295952
  1232.8 137.8 %reduce-scatter.16.cloned.1.call-done = bf16[136,1088]{1,0:T(8,128)(2,1)} async-done(((bf16[4352,1088]{1,0:T(8,128)(2,1)}), bf16[136,1088]{1,0:T(8,128)(2,1)}) %reduce-scatter.16.cloned.1.call-update) | async-done | bytes 295952
  1370.7 13.8 fusion.57
  1384.5 43.7 %all-gather.31.cloned.1.call-done = f32[32,4,3264]{2,1,0:T(4,128)} async-done(((f32[1,4,3264]{2,1,0:T(4,128)}), f32[32,4,3264]{2,1,0:T(4,128)}) %all-gather.31.cloned.1.call-update) | async-done | bytes 1671184 | tf_op jit(solution)/shard_map/all_gather | solution.py:253
  1431.8 26.5 %all-gather.23.cloned.1.call-done = bf16[1088,1088]{1,0:T(8,128)(2,1)} async-done(((bf16[136,1088]{1,0:T(8,128)(2,1)}), bf16[1088,1088]{1,0:T(8,128)(2,1)}) %all-gather.23.cloned.1.call-update) | async-done | bytes 2367504 | tf_op jit(solution)/shard_map/all_gather | solution.py:229
  1460.4 4.2 copy.85
  1464.6 6.6 reshape.504
  1471.2 18.5 %all-gather.25.cloned.1.call-done = bf16[1088,1088]{1,0:T(8,128)(2,1)} async-done(((bf16[136,1088]{1,0:T(8,128)(2,1)}), bf16[1088,1088]{1,0:T(8,128)(2,1)}) %all-gather.25.cloned.1.call-update) | async-done | bytes 2367504 | tf_op jit(solution)/shard_map/all_gather | solution.py:229
  1489.8 4.3 convert_element_type.291
  1494.1 26.9 %all-gather.21.cloned.1.call-done = bf16[1088,1088]{1,0:T(8,128)(2,1)} async-done(((bf16[136,1088]{1,0:T(8,128)(2,1)}), bf16[1088,1088]{1,0:T(8,128)(2,1)}) %all-gather.21.cloned.1.call-update) | async-done | bytes 2367504 | tf_op jit(solution)/shard_map/all_gather | solution.py:229
  1525.7 6.7 reshape.503
  (423 shorter events, 373.9 us)
Async XLA Ops:
  7.2 146.6 %copy-start = (bf16[1088,1088]{1,0:T(8,128)(2,1)S(1)}, bf16[1088,1088]{1,0:T(8,128)(2,1)}, u32[]{:S(2)}) copy-start(bf16[1088,1088]{1,0:T(8,128)(2,1)} %param.25) | copy-start | bytes 7102468
  7.2 6.0 copy-start.20
  7.2 102.0 %all-gather.15.cloned.1.call-start = ((), (), s32[]{:S(2)}) async-start(), calls=%async_computation.5 | async-start | bytes 10340352 | tf_op jit(solution)/shard_map/all_gather | solution.py:51
  22.0 173.3 %all-gather.17.cloned.1.call-start = ((), (), s32[]{:S(2)}) async-start(), calls=%async_computation.6 | async-start | bytes 10340352 | tf_op jit(solution)/shard_map/all_gather | solution.py:51
  28.3 3.0 copy-start.40
  28.4 4.2 copy-start.32
  28.4 4.2 copy-start.33
  28.4 4.2 copy-start.34
  28.4 4.3 copy-start.35
  28.4 4.2 copy-start.36
  28.4 4.2 copy-start.37
  28.4 4.2 copy-start.38
  28.4 4.2 copy-start.39
  31.3 249.8 %all-gather.27.cloned.1.call-start = ((), (), s32[]{:S(2)}) async-start(), calls=%async_computation.13 | async-start | bytes 5570560 | tf_op jit(solution)/shard_map/all_gather | solution.py:92
  55.0 88.0 %copy-start.21 = (f32[1088]{0:T(1024)}, f32[1088]{0:T(1024)S(1)}, u32[]{:S(2)}) copy-start(f32[1088]{0:T(1024)S(1)} %reshape.496) | copy-start | bytes 13060
  55.3 87.7 %copy-start.30 = (f32[1088]{0:T(1024)}, f32[1088]{0:T(1024)S(1)}, u32[]{:S(2)}) copy-start(f32[1088]{0:T(1024)S(1)} %reshape.497) | copy-start | bytes 13060
  56.9 86.1 %copy-start.23 = (f32[512]{0:T(512)}, f32[512]{0:T(512)S(1)}, u32[]{:S(2)}) copy-start(f32[512]{0:T(512)S(1)} %broadcast_multiply_fusion.1) | copy-start | bytes 6148
  58.5 54.4 %copy-start.26 = (f32[512]{0:T(512)}, f32[512]{0:T(512)S(1)}, u32[]{:S(2)}) copy-start(f32[512]{0:T(512)S(1)} %fusion.64) | copy-start | bytes 6148
  58.5 84.5 %copy-start.28 = (f32[512]{0:T(512)}, f32[512]{0:T(512)S(1)}, u32[]{:S(2)}) copy-start(f32[512]{0:T(512)S(1)} %fusion.77) | copy-start | bytes 6148
  153.2 213.4 %all-gather.29.cloned.1.call-start = ((), (), s32[]{:S(2)}) async-start(), calls=%async_computation.14 | async-start | bytes 5570560 | tf_op jit(solution)/shard_map/all_gather | solution.py:93
  153.8 376.5 %all-gather.19.cloned.1.call-start = ((), (), s32[]{:S(2)}) async-start(), calls=%async_computation.7 | async-start | bytes 10340352 | tf_op jit(solution)/shard_map/all_gather | solution.py:51
  154.6 4.1 copy-start.11
  154.6 716.2 %reduce-scatter.12.cloned.1.call-start = ((), (), s32[]{:S(2)}) async-start(), calls=%async_computation.8 | async-start | bytes 5570560 | tf_op jit(solution)/shard_map/reduce_scatter | solution.py:206
  374.2 118.0 %copy-start.4 = (bf16[1,512,1088]{1,2,0:T(8,128)(2,1)S(1)}, bf16[1,512,1088]{1,2,0:T(8,128)(2,1)}, u32[]{:S(2)}) copy-start(bf16[1,512,1088]{1,2,0:T(8,128)(2,1)} %param.18) | copy-start | bytes 3342340
  492.2 4.2 copy-start.10
  497.8 32.5 %copy-start.12 = (bf16[1,512,1088]{1,2,0:T(8,128)(2,1)S(1)}, bf16[1,512,1088]{1,2,0:T(8,128)(2,1)}, u32[]{:S(2)}) copy-start(bf16[1,512,1088]{1,2,0:T(8,128)(2,1)} %param.31) | copy-start | bytes 3342340
  530.3 18.0 %copy-start.8 = (f32[512,1088]{0,1:T(8,128)S(1)}, f32[512,1088]{0,1:T(8,128)}, u32[]{:S(2)}) copy-start(f32[512,1088]{0,1:T(8,128)} %copy-done.7) | copy-start | bytes 6684676
  558.9 5.6 copy-start.2
  558.9 3.0 copy-start.16
  560.0 4.6 copy-start.17
  791.1 163.5 %reduce-scatter.14.cloned.1.call-start = ((), (), s32[]{:S(2)}) async-start(), calls=%async_computation.9 | async-start | bytes 5570560 | tf_op jit(solution)/shard_map/reduce_scatter | solution.py:207
  791.9 302.6 %reduce-scatter.18.cloned.1.call-start = ((), (), s32[]{:S(2)}) async-start(), calls=%async_computation.17 | async-start | bytes 10340352
  830.4 402.3 %reduce-scatter.20.cloned.1.call-start = ((), (), s32[]{:S(2)}) async-start(), calls=%async_computation.18 | async-start | bytes 10340352
  843.4 527.1 %reduce-scatter.16.cloned.1.call-start = ((), (), s32[]{:S(2)}) async-start(), calls=%async_computation.16 | async-start | bytes 10340352
  849.0 105.7 %copy-start.5 = (bf16[1,512,1088]{1,2,0:T(8,128)(2,1)S(1)}, bf16[1,512,1088]{1,2,0:T(8,128)(2,1)}, u32[]{:S(2)}) copy-start(bf16[1,512,1088]{1,2,0:T(8,128)(2,1)} %param.18) | copy-start | bytes 3342340
  849.0 105.7 %copy-start.22 = (f32[1088]{0:T(1024)S(1)}, f32[1088]{0:T(1024)}, u32[]{:S(2)}) copy-start(f32[1088]{0:T(1024)} %copy-done.21) | copy-start | bytes 13060
  849.0 105.7 %copy-start.24 = (f32[512]{0:T(512)S(1)}, f32[512]{0:T(512)}, u32[]{:S(2)}) copy-start(f32[512]{0:T(512)} %copy-done.23) | copy-start | bytes 6148
  849.0 105.7 %copy-start.29 = (f32[512]{0:T(512)S(1)}, f32[512]{0:T(512)}, u32[]{:S(2)}) copy-start(f32[512]{0:T(512)} %copy-done.28) | copy-start | bytes 6148
  849.0 105.7 %copy-start.31 = (f32[1088]{0:T(1024)S(1)}, f32[1088]{0:T(1024)}, u32[]{:S(2)}) copy-start(f32[1088]{0:T(1024)} %copy-done.30) | copy-start | bytes 13060
  1005.7 422.5 %all-gather.31.cloned.1.call-start = ((), (), s32[]{:S(2)}) async-start(), calls=%async_computation.15 | async-start | bytes 1757184 | tf_op jit(solution)/shard_map/all_gather | solution.py:253
  1009.7 8.0 copy-start.27
  1009.7 8.0 copy-start.6
  1017.6 2.0 copy-start.15
  1019.6 351.0 %copy-start.25 = (f32[4,272]{1,0:T(4,128)S(1)}, f32[4,272]{1,0:T(4,128)}, u32[]{:S(2)}) copy-start(f32[4,272]{1,0:T(4,128)} %get-tuple-element.307) | copy-start | bytes 13060
  1023.1 435.3 %all-gather.23.cloned.1.call-start = ((), (), s32[]{:S(2)}) async-start(), calls=%async_computation.11 | async-start | bytes 2820096 | tf_op jit(solution)/shard_map/all_gather | solution.py:229
  1094.5 395.2 %all-gather.25.cloned.1.call-start = ((), (), s32[]{:S(2)}) async-start(), calls=%async_computation.12 | async-start | bytes 2820096 | tf_op jit(solution)/shard_map/all_gather | solution.py:229
  1232.7 288.3 %all-gather.21.cloned.1.call-start = ((), (), s32[]{:S(2)}) async-start(), calls=%async_computation.10 | async-start | bytes 2820096 | tf_op jit(solution)/shard_map/all_gather | solution.py:229
  1525.7 8.9 copy-start.1
  (8 other events, 11.2 us)
Sparse Core Ops, SparseCore 0:
  22.1 86.9 all-gather.14
  112.7 82.5 all-gather.16
  197.4 83.5 all-gather.26
  283.1 83.4 all-gather.28
  369.4 82.4 all-gather.18
  791.3 79.4 reduce-scatter.11
  873.1 81.5 reduce-scatter.13
  960.8 133.7 reduce-scatter.17
  1100.6 132.0 reduce-scatter.19
  1238.7 131.8 reduce-scatter.15
  1374.0 54.0 all-gather.30
  1429.9 28.4 all-gather.22
  1460.2 29.4 all-gather.24
  1491.5 29.4 all-gather.20
